TPU v7x, 32 devices: a whole 2x2x4 slice. The times are simulated.
32 devices in a mesh: groups: 2 (over y), gy: 4 (over z), gz: 4 (over x, core).
Axes of the slice: x: 2, y: 2, z: 4, core: 2. Of those that a mesh axis runs over, the one named last changes fastest.
Arguments:
- indirect: float32 [4, 512, 32, 512], P('groups', 'gy', 'gz'), parts along dimension 0, may hold values from -6 to 6
- past_indirect: float32 [8, 2, 512, 32, 512], P('groups', None, 'gy', 'gz'), parts along dimension 0, may hold values from -6 to 6
- past_residual: float32 [8, 2, 512, 32, 512], P('groups', None, 'gy', 'gz'), parts along dimension 0, may hold values from -40 to 40
- atom_table: float32 [10, 4, 4, 128], P('groups', 'gy', 'gz'), parts along dimension 0, may hold values from -4 to 512, as said below
- atom_counts: int32 [8, 4], P(('groups', 'gy'), 'gz'), parts along dimension 0, may hold values from 1 to 128, as said below
- chi_amps: float32 [3, 4], replicated, may hold values from -3 to 3
- chi_widths: float32 [4], replicated, may hold values from 0.5 to 4
Outputs:
- new_indirect: float32 [4, 512, 32, 512], P('groups', 'gy', 'gz'), parts along dimension 0
- residual: float32 [4, 512, 32, 512], P('groups', 'gy', 'gz'), parts along dimension 0
There are 2 independent parts, one for each index of `groups`. A program takes and returns all parts, laid end to end along the dimension named above; an argument that names none is the same for every part. Nothing has to cross between parts.
Inputs may be any that keep to these rules, and one draw needn't show every extreme that they name: `atom_counts`: some pencil has exactly 128 live rows in every draw. `atom_table`: each row of pencil (p, q) has its y position in [p * 128, (p + 1) * 128) and its z position in [q * 8, (q + 1) * 8); x positions lie in [0, 512).
All inputs are finite; a program needn't handle non-finite values.
Results may differ from a plain program's by a relative error of at most 0.0003.
Values sent between devices are 32-bit elements; how exact they have to be, the bound alone decides.
A program may use at most 192 MiB of HBM per device.

v0:
```python
import math
import jax
import jax.numpy as jnp
from jax import lax
from jax.sharding import PartitionSpec as P

SIGX = 8
PRECISE = lax.Precision.HIGHEST
MIX_STEP = 0.3
BOND_OH = 1.9
BOND_HH = 3.1


def with_halo(cells, sides, width):
    for axis, dim in sides:
        count = lax.axis_size(axis)
        head = lax.slice_in_dim(cells, 0, width, axis=dim)
        tail = lax.slice_in_dim(cells, cells.shape[dim] - width, cells.shape[dim], axis=dim)
        cells = jnp.concatenate(
            [
                lax.ppermute(tail, axis, [(i, (i + 1) % count) for i in range(count)]),
                cells,
                lax.ppermute(head, axis, [((i + 1) % count, i) for i in range(count)]),
            ],
            axis=dim,
        )
    return cells


def hartley(length):
    position = lax.iota(jnp.int32, length)
    product = position[:, None] * position[None, :] % length
    angle = product.astype(jnp.float32) * (2.0 * math.pi / length)
    return (jnp.cos(angle) + jnp.sin(angle)) / math.sqrt(length)


def wave_squared(position, length):
    folded = jnp.where(2 * position > length, position - length, position)
    scaled = folded.astype(jnp.float32) * (2.0 * math.pi / length)
    return scaled * scaled


def response(wave_square, chi_amps, chi_widths):
    wavenumber = jnp.sqrt(wave_square)
    summed = [jnp.zeros_like(wave_square) for channel in range(3)]
    for which_term in range(chi_widths.shape[0]):
        gaussian_term = jnp.exp(-wave_square * (chi_widths[which_term] * chi_widths[which_term]))
        summed = [
            summed[channel] + chi_amps[channel, which_term] * gaussian_term for channel in range(3)
        ]
    oxygen = 1.0 + summed[0]
    mixed_site = 2.0 * jnp.sinc(wavenumber * (BOND_OH / math.pi)) + summed[1]
    hydrogen = 2.0 + 2.0 * jnp.sinc(wavenumber * (BOND_HH / math.pi)) + summed[2]
    return (oxygen, mixed_site, hydrogen)


def couple(spectrum, wave_square, chi_amps, chi_widths):
    oxygen, mixed_site, hydrogen = response(wave_square, chi_amps, chi_widths)
    return jnp.stack(
        [
            oxygen * spectrum[0] + mixed_site * spectrum[1],
            mixed_site * spectrum[0] + hydrogen * spectrum[1],
        ]
    )


def gaussian(offset, length, spread):
    offset = offset - length * jnp.floor(offset / length + 0.5)
    return jnp.exp(-0.5 * offset * offset / (spread * spread))


def pencil_field(
    atom_rows, pencil_y, pencil_z, cells_y, cells_z, total_x, total_y, total_z, spread_x
):
    cell_y = (pencil_y * cells_y + lax.iota(jnp.int32, cells_y)).astype(jnp.float32)
    cell_z = (pencil_z * cells_z + lax.iota(jnp.int32, cells_z)).astype(jnp.float32)
    cell_x = lax.iota(jnp.int32, total_x).astype(jnp.float32)
    along_y = gaussian(cell_y[:, None] - atom_rows[1][None, :], total_y, 0.5 * cells_y)
    along_z = gaussian(cell_z[:, None] - atom_rows[2][None, :], total_z, 0.5 * cells_z)
    along_x = gaussian(cell_x[:, None] - atom_rows[0][None, :], total_x, spread_x)
    left = atom_rows[3:5][:, None, None, :] * along_y[None, :, None, :] * along_z[None, None, :, :]
    left = left.reshape(2, cells_y * cells_z, atom_rows.shape[1])
    return jnp.einsum("sra,xa->srx", left, along_x, precision=PRECISE)


def body(indirect, past_indirect, past_residual, atom_table, atom_counts, chi_amps, chi_widths):
    cells_y = indirect.shape[1]
    cells_z = indirect.shape[2]
    cells_x = indirect.shape[3]
    parts_y = lax.axis_size("gy")
    parts_z = lax.axis_size("gz")
    total_y = cells_y * parts_y
    total_z = cells_z * parts_z
    row_count = atom_table.shape[3]
    present = (lax.iota(jnp.int32, row_count) < atom_counts[0, 0]).astype(jnp.float32)
    bucket = jnp.concatenate([atom_table[0:3], atom_table[3:5] * present], 0)
    nearby = with_halo(bucket, (("gy", 1), ("gz", 2)), 1)
    nearby = nearby.reshape(5, 9 * row_count)
    potential_field = pencil_field(
        nearby,
        lax.axis_index("gy"),
        lax.axis_index("gz"),
        cells_y,
        cells_z,
        cells_x,
        total_y,
        total_z,
        float(SIGX),
    )
    potential_field = potential_field.reshape(2, cells_y, cells_z, cells_x)
    argument = indirect - potential_field
    closed = jnp.where(argument > 0, argument, jnp.expm1(jnp.minimum(argument, 0.0)))
    direct = closed - indirect
    table_x = hartley(cells_x)
    table_y = hartley(total_y)
    table_z = hartley(total_z)
    blocks = parts_y * parts_z
    width_x = cells_x // blocks
    grid_y = table_y.reshape(parts_y, cells_y, total_y)
    grid_z = table_z.reshape(parts_z, cells_z, total_z)
    outgoing = jnp.einsum(
        "scdx,xqk->sqkdc", direct, table_x.reshape(cells_x, blocks, width_x), precision=PRECISE
    )
    outgoing = outgoing.reshape(2, blocks, 1, width_x * cells_z * cells_y)
    received = lax.all_to_all(outgoing, ("gy", "gz"), split_axis=1, concat_axis=2, tiled=True)
    count = received.shape[0]
    pieces = received.reshape(count, parts_y, parts_z, width_x, cells_z, cells_y)
    partial_value = jnp.einsum("sabxdc,acy->sbxdy", pieces, grid_y, precision=PRECISE)
    section_two = jnp.einsum("sbxdy,bdz->sxzy", partial_value, grid_z, precision=PRECISE)
    wave_x = wave_squared(
        lax.axis_index(("gy", "gz")) * width_x + lax.iota(jnp.int32, width_x), cells_x
    )
    wave_square = (
        wave_x[:, None, None]
        + wave_squared(lax.iota(jnp.int32, total_z), total_z)[None, :, None]
        + wave_squared(lax.iota(jnp.int32, total_y), total_y)[None, None, :]
    )
    coupled = couple(section_two, wave_square, chi_amps, chi_widths)
    partial_value = jnp.einsum("sxzy,bdz->sxbdy", coupled, grid_z, precision=PRECISE)
    returning = jnp.einsum("sxbdy,acy->sabxdc", partial_value, grid_y, precision=PRECISE)
    returning = returning.reshape(2, blocks, 1, width_x * cells_z * cells_y)
    table_back = table_x.reshape(blocks, width_x, cells_x)
    received = lax.all_to_all(returning, ("gy", "gz"), split_axis=1, concat_axis=2, tiled=True)
    count = received.shape[0]
    pieces = received.reshape(count, blocks, width_x, cells_z, cells_y)
    summed_field = jnp.einsum("sqxdc,qxk->scdk", pieces, table_back, precision=PRECISE)
    residual = summed_field - direct - indirect
    stacked = jnp.concatenate([residual[None], past_residual], 0)
    gram_matrix = jnp.einsum("isyzx,jsyzx->ij", stacked, stacked, precision=PRECISE)
    gram_matrix = lax.psum(gram_matrix, ("gy", "gz"))
    factor = jnp.linalg.cholesky(gram_matrix)
    weights = jax.scipy.linalg.cho_solve(
        (factor, True), jnp.ones((gram_matrix.shape[0],), jnp.float32)
    )
    mixing = weights / jnp.sum(weights)
    earlier = jnp.einsum(
        "i,isyzx->syzx", mixing[1:], past_indirect + MIX_STEP * past_residual, precision=PRECISE
    )
    new_indirect = mixing[0] * (indirect + MIX_STEP * residual) + earlier
    return (new_indirect, residual)


def solution(mesh):
    return jax.shard_map(
        body,
        mesh=mesh,
        in_specs=(
            P("groups", "gy", "gz", None),
            P("groups", None, "gy", "gz", None),
            P("groups", None, "gy", "gz", None),
            P("groups", "gy", "gz", None),
            P(("groups", "gy"), "gz"),
            P(),
            P(),
        ),
        out_specs=(P("groups", "gy", "gz", None), P("groups", "gy", "gz", None)),
        check_vma=False,
    )
```

profile of v0, /device:TPU:0, one launch (start us, length us, event | category | flops | bytes accessed | tf_op | source)
XLA Modules:
  0.0 549.4 jit_solution(14519221556603764568)
XLA Ops:
  13.1 18.8 %fusion.6 = f32[2,128,8,512]{3,1,2,0:T(8,128)S(1)} fusion(f32[8,1152]{1,0:T(8,128)S(1)} %fusion.224, f32[2,128,1152]{2,1,0:T(8,128)S(1)} %broadcast_multiply_fusion, f32[1152]{0:T(1024)S(1)} %sub.111, f32[512]{0:T(512)S(1)} %iota_convert_fusion), kind=kOutput, calls=%fused_computation.8 | convolution fusion | flops 14503182336 | bytes 5417472 | tf_op jit(solution)/shard_map/sra,xa->srx/dot_general | solution.py:83
  31.9 14.1 %fusion.56 = f32[2,16,32,8,128]{4,2,3,0,1:T(8,128)S(1)} fusion(f32[2,128,8,512]{3,1,2,0:T(8,128)S(1)} %fusion.6, f32[2,128,8,512]{3,2,1,0:T(8,128)S(1)} %copy-done.2, s32[16,32]{1,0:T(8,128)S(1)} %multiply_add_fusion.3), kind=kOutput, calls=%fused_computation.68 | convolution fusion | flops 6451888128 | bytes 12584960 | tf_op jit(solution)/shard_map/scdx,xqk->sqkdc/dot_general | solution.py:121
  46.0 5.8 %copy.90 = f32[2,16,32,8,128]{4,3,2,0,1:T(8,128)} copy(f32[2,16,32,8,128]{4,2,3,0,1:T(8,128)S(1)} %fusion.56) | data formatting | bytes 8388608 | tf_op jit(solution)/shard_map/reshape | solution.py:124
  51.8 5.9 %reshape.439 = f32[2,16,1,32768]{3,0,2,1:T(2,128)} reshape(f32[2,16,32,8,128]{4,3,2,0,1:T(8,128)} %copy.90) | data formatting | bytes 8388608 | tf_op jit(solution)/shard_map/reshape | solution.py:124
  57.8 6.7 %all-to-all-start = ((f32[2,16,1,32768]{3,0,2,1:T(2,128)}), f32[2,16,1,32768]{3,0,2,1:T(2,128)}, u32[]{:S(2)}, u32[]{:S(2)}) async-start(f32[2,16,1,32768]{3,0,2,1:T(2,128)} %reshape.439), calls=%async_computation | async-start | bytes 8388608 | tf_op jit(solution)/shard_map/all_to_all | solution.py:125
  71.0 71.0 %all-to-all-done = f32[2,16,1,32768]{3,0,2,1:T(2,128)} async-done(((f32[2,16,1,32768]{3,0,2,1:T(2,128)}), f32[2,16,1,32768]{3,0,2,1:T(2,128)}, u32[]{:S(2)}, u32[]{:S(2)}) %all-to-all-start) | async-done | bytes 4194336 | tf_op jit(solution)/shard_map/all_to_all | solution.py:125
  142.1 7.0 %reshape.440 = f32[2,4,4,32,8,128]{5,4,3,0,2,1:T(8,128)} reshape(f32[2,16,1,32768]{3,0,2,1:T(2,128)} %all-to-all-done) | data formatting | bytes 8388608 | tf_op jit(solution)/shard_map/reshape | solution.py:127
  149.1 13.7 %fusion.21 = f32[2,4,32,8,512,1]{4,3,5,1,2,0:T(8,128)S(1)} fusion(f32[2,4,4,32,8,128]{5,4,3,0,2,1:T(8,128)} %reshape.440, s32[4,128]{1,0:T(4,128)S(1)} %multiply_add_fusion.5), kind=kOutput, calls=%fused_computation.26 | convolution fusion | flops 6446645248 | bytes 8390656 | tf_op jit(solution)/shard_map/sabxdc,acy->sbxdy/dot_general | solution.py:128
  167.2 12.9 %fusion.101 = f32[1,32,32,512]{3,2,1,0:T(8,128)S(1)} fusion(f32[2,32,32,512]{3,2,1,0:T(8,128)S(1)} %fusion.59, f32[]{:T(128)} %bitcast.42, f32[]{:T(128)} %bitcast.41, f32[]{:T(128)} %bitcast.40, f32[]{:T(128)} %bitcast.39, f32[]{:T(128)} %bitcast.14, f32[]{:T(128)} %bitcast.12, f32[]{:T(128)} %bitcast.10, f32[]{:T(128)} %bitcast.8, f32[512]{0:T(512)S(1)} %fusion.240, ...), kind=kLoop, calls=%fused_computation.107 | loop fusion | flops 50331648 | bytes 6297648 | tf_op jit(solution)/shard_map/stack | solution.py:59
  180.0 10.3 %fusion.90 = f32[1,32,32,512]{3,2,1,0:T(8,128)S(1)} fusion(f32[2,32,32,512]{3,2,1,0:T(8,128)S(1)} %fusion.59, f32[]{:T(128)} %bitcast.14, f32[]{:T(128)} %bitcast.13, f32[]{:T(128)} %bitcast.12, f32[]{:T(128)} %bitcast.11, f32[]{:T(128)} %bitcast.10, f32[]{:T(128)} %bitcast.9, f32[]{:T(128)} %bitcast.8, f32[512]{0:T(512)S(1)} %fusion.240, ...), kind=kLoop, calls=%fused_computation.96 | loop fusion | flops 31457280 | bytes 6297648 | tf_op jit(solution)/shard_map/stack | solution.py:59
  194.5 13.6 %fusion.63 = f32[2,4,4,32,8,128]{5,3,4,2,0,1:T(8,128)S(1)} fusion(f32[2,32,4,8,512]{4,3,1,0,2:T(8,128)S(1)} %fusion.62, s32[4,128]{1,0:T(4,128)S(1)} %multiply_add_fusion.5), kind=kOutput, calls=%fused_computation.71 | convolution fusion | flops 6446645248 | bytes 8390656 | tf_op jit(solution)/shard_map/sxbdy,acy->sabxdc/dot_general | solution.py:140
  208.0 5.8 %copy.93 = f32[2,4,4,32,8,128]{5,4,3,0,2,1:T(8,128)} copy(f32[2,4,4,32,8,128]{5,3,4,2,0,1:T(8,128)S(1)} %fusion.63) | data formatting | bytes 8388608 | tf_op jit(solution)/shard_map/reshape | solution.py:141
  213.8 5.9 %reshape.441 = f32[2,16,1,32768]{3,0,2,1:T(2,128)} reshape(f32[2,4,4,32,8,128]{5,4,3,0,2,1:T(8,128)} %copy.93) | data formatting | bytes 8388608 | tf_op jit(solution)/shard_map/reshape | solution.py:141
  219.7 19.7 %all-to-all-start.1 = ((f32[2,16,1,32768]{3,0,2,1:T(2,128)}), f32[2,16,1,32768]{3,0,2,1:T(2,128)}, u32[]{:S(2)}, u32[]{:S(2)}) async-start(f32[2,16,1,32768]{3,0,2,1:T(2,128)} %reshape.441), calls=%async_computation.1 | async-start | bytes 8388608 | tf_op jit(solution)/shard_map/all_to_all | solution.py:143
  239.4 18.3 %copy.69 = f32[4,2,128,8,512]{2,0,3,4,1:T(4,128)} copy(f32[4,2,128,8,512]{4,3,2,1,0:T(8,128)} %param.10) | data formatting | bytes 33554432 | tf_op args[2]
  257.7 17.5 %multiply_add_fusion = f32[4,2,128,8,512]{4,3,2,1,0:T(8,128)} fusion(f32[4,2,128,8,512]{4,3,2,1,0:T(8,128)} %param.9, f32[4,2,128,8,512]{4,3,2,1,0:T(8,128)} %param.10), kind=kLoop, calls=%fused_computation.6 | loop fusion | flops 8388608 | bytes 50331648 | tf_op jit(solution)/shard_map/add | solution.py:157
  275.2 41.7 %all-to-all-done.1 = f32[2,16,1,32768]{3,0,2,1:T(2,128)} async-done(((f32[2,16,1,32768]{3,0,2,1:T(2,128)}), f32[2,16,1,32768]{3,0,2,1:T(2,128)}, u32[]{:S(2)}, u32[]{:S(2)}) %all-to-all-start.1) | async-done | bytes 4194336 | tf_op jit(solution)/shard_map/all_to_all | solution.py:143
  317.0 6.6 %reshape.442 = f32[2,16,32,8,128]{4,3,2,0,1:T(8,128)} reshape(f32[2,16,1,32768]{3,0,2,1:T(2,128)} %all-to-all-done.1) | data formatting | bytes 8388608 | tf_op jit(solution)/shard_map/reshape | solution.py:145
  323.6 26.4 %fusion.14 = f32[2,128,8,512]{3,1,2,0:T(8,128)S(1)} fusion(f32[2,128,8,512]{3,2,1,0:T(8,128)} %param.8, f32[2,128,8,512]{3,1,2,0:T(8,128)} %copy-done.6, f32[2,16,32,8,128]{4,3,2,0,1:T(8,128)} %reshape.442, s32[16,32]{1,0:T(8,128)S(1)} %multiply_add_fusion.3), kind=kOutput, calls=%fused_computation.18 | convolution fusion | flops 6453985280 | bytes 16779264 | tf_op jit(solution)/shard_map/sqxdc,qxk->scdk/dot_general | solution.py:146
  354.4 11.0 %copy.68 = f32[1,2,128,8,512]{2,0,3,4,1:T(1,128)} copy(f32[1,2,128,8,512]{4,2,3,1,0:T(8,128)} %bitcast.155) | data formatting | bytes 8388608 | tf_op jit(solution)/shard_map/broadcast_in_dim | solution.py:148
  365.4 76.1 %fusion.132 = f32[5,5]{0,1:T(8,128)S(1)} fusion(f32[4,2,128,8,512]{2,0,3,4,1:T(4,128)} %copy.69, f32[1,2,128,8,512]{2,0,3,4,1:T(1,128)} %copy.68), kind=kOutput, calls=%fused_computation.158 | convolution fusion | flops 319815680 | bytes 20971620 | tf_op jit(solution)/shard_map/isyzx,jsyzx->ij/dot_general | solution.py:149
  441.5 47.8 %psum.7 = f32[5,5]{0,1:T(8,128)S(1)} all-reduce(f32[5,5]{0,1:T(8,128)S(1)} %fusion.132), channel_id=1, replica_groups=mesh['groups'=2,'gy'=4,'gz'=4] {'gy','gz'}, use_global_device_ids=true, to_apply=%region_0.2 | all-reduce | flops 25 | bytes 200 | tf_op jit(solution)/shard_map/psum | solution.py:150
  492.8 46.8 %fusion.4 = f32[1,2,128,8,512]{4,0,3,2,1:T(1,128)S(1)} fusion(f32[4,2,128,8,512]{4,3,2,1,0:T(8,128)} %multiply_add_fusion, f32[5]{0:T(128)S(1)} %broadcast_divide_fusion), kind=kOutput, calls=%fused_computation.4 | convolution fusion | flops 50331648 | bytes 20971540 | tf_op jit(solution)/shard_map/i,isyzx->syzx/dot_general | solution.py:156
  539.6 5.1 bitcast_add_fusion
  (62 shorter events, 34.0 us)
Async XLA Ops:
  2.7 6.7 %collective-permute-start = (f32[5,1,1,128]{3,2,1,0:T(1,128)S(1)}, f32[5,1,1,128]{3,2,1,0:T(1,128)S(1)}, u32[]{:S(2)}, u32[]{:S(2)}) collective-permute-start(f32[5,1,1,128]{3,2,1,0:T(1,128)S(1)} %pad_maximum_fusion.5), channel_id=1, source_target_pairs={{0,4},{4,8},{8,12},{12,0},{1,5},{5,9},{9,13},{13,1},{2,6},{6,10},{... | collective-permute-start | bytes 7688 | tf_op jit(solution)/shard_map/ppermute | solution.py:21
  5.7 3.6 collective-permute-start.1
  9.3 3.1 collective-permute-start.2
  9.4 3.1 collective-permute-start.3
  13.1 18.8 %copy-start.2 = (f32[2,128,8,512]{3,2,1,0:T(8,128)S(1)}, f32[2,128,8,512]{3,2,1,0:T(8,128)}, u32[]{:S(2)}) copy-start(f32[2,128,8,512]{3,2,1,0:T(8,128)} %param.8) | copy-start | bytes 12582916
  31.9 14.1 %copy-start.6 = (f32[2,128,8,512]{3,1,2,0:T(8,128)}, f32[2,128,8,512]{3,1,2,0:T(8,128)S(1)}, u32[]{:S(2)}) copy-start(f32[2,128,8,512]{3,1,2,0:T(8,128)S(1)} %fusion.6) | copy-start | bytes 12582916
  57.7 6.8 %copy-start.5 = (f32[4]{0:T(128)S(1)}, f32[4]{0:T(128)}, u32[]{:S(2)}) copy-start(f32[4]{0:T(128)} %param.14) | copy-start | bytes 52
  57.8 12.5 %copy-start.4 = (f32[3,4]{1,0:T(4,128)S(1)}, f32[3,4]{1,0:T(4,128)}, u32[]{:S(2)}) copy-start(f32[3,4]{1,0:T(4,128)} %param.13) | copy-start | bytes 148
  57.8 84.3 %all-to-all-start = ((f32[2,16,1,32768]{3,0,2,1:T(2,128)}), f32[2,16,1,32768]{3,0,2,1:T(2,128)}, u32[]{:S(2)}, u32[]{:S(2)}) async-start(f32[2,16,1,32768]{3,0,2,1:T(2,128)} %reshape.439), calls=%async_computation | async-start | bytes 8388608 | tf_op jit(solution)/shard_map/all_to_all | solution.py:125
  219.7 97.2 %all-to-all-start.1 = ((f32[2,16,1,32768]{3,0,2,1:T(2,128)}), f32[2,16,1,32768]{3,0,2,1:T(2,128)}, u32[]{:S(2)}, u32[]{:S(2)}) async-start(f32[2,16,1,32768]{3,0,2,1:T(2,128)} %reshape.441), calls=%async_computation.1 | async-start | bytes 8388608 | tf_op jit(solution)/shard_map/all_to_all | solution.py:143
  350.0 4.5 copy-start
  492.8 46.8 %copy-start.1 = (f32[2,128,8,512]{3,1,2,0:T(8,128)S(1)}, f32[2,128,8,512]{3,1,2,0:T(8,128)}, u32[]{:S(2)}) copy-start(f32[2,128,8,512]{3,1,2,0:T(8,128)} %copy-done) | copy-start | bytes 12582916
  492.8 46.8 %copy-start.3 = (f32[2,128,8,512]{3,2,1,0:T(8,128)S(1)}, f32[2,128,8,512]{3,2,1,0:T(8,128)}, u32[]{:S(2)}) copy-start(f32[2,128,8,512]{3,2,1,0:T(8,128)} %param.8) | copy-start | bytes 12582916
where the time goes:
time: 558 us; the launch traced here: 549 us
  matrix products  219 us (39%)
  waiting for transfers between devices  116 us (21%)
  local copies, waits for them, and re-layouts  77.4 us (14%)
  other arithmetic  49.8 us (9%)
  blocking collectives  47.8 us (9%)
  starting transfers between devices  33.4 us (6%)
  between operations  6.84 us (1%)
    dot_general x1, matrix products, body(): jnp.einsum('isyzx,jsyzx->ij', stacked, stacked, precision=PRECISE)  76.1 us
    all_to_all x1, waiting for transfers between devices, body(): lax.all_to_all(outgoing, ('gy', 'gz'), split_axis=1, concat_axis=2, tiled...  71 us
    psum x1, blocking collectives, body(): gram_matrix = lax.psum(gram_matrix, ('gy', 'gz'))  47.8 us
    dot_general x1, matrix products, body(): jnp.einsum('i,isyzx->syzx', mixing[1:], past_indirect + MIX_STEP * past_r...  46.8 us
    all_to_all x1, waiting for transfers between devices, body(): lax.all_to_all(returning, ('gy', 'gz'), split_axis=1, concat_axis=2, tile...  41.7 us
    unnamed x17, local copies, waits for them, and re-layouts  27.2 us
    dot_general x1, matrix products, body(): jnp.einsum('sqxdc,qxk->scdk', pieces, table_back, precision=PRECISE)  26.4 us
    another operation x2, other arithmetic, couple(): jnp.stack([oxygen * spectrum[0] + mixed_site * spectrum[1], mixed_site *...  23.2 us
  transfers between devices with their start and end apart: 6, of which 4 were waited for; matrix products, arithmetic and copies ran while one was open for 7% of the time, Pallas kernels for 0%

commit v1 on v0

--- a/solution.py
+++ b/solution.py
@@ -9,6 +9,29 @@
 MIX_STEP = 0.3
 BOND_OH = 1.9
 BOND_HH = 3.1
+
+
+def in_blocks(shard, dim, length):
+    dims = shard.shape
+    pieces = shard.reshape(*dims[:dim], length, dims[dim] // length, *dims[dim + 1 :])
+    return jnp.moveaxis(pieces, dim, 0)
+
+
+def joined_along(blocks, dim):
+    dims = list(blocks.shape[1:])
+    dims[dim] *= blocks.shape[0]
+    return jnp.moveaxis(blocks, 0, dim).reshape(dims)
+
+
+def exchange_in_pairs(value, axis, split_dim, concat_dim):
+    size, index = (lax.axis_size(axis), lax.axis_index(axis))
+    tiles = in_blocks(value, split_dim, size)
+    done = [tiles[index]]
+    for hop in range(1, size):
+        sent = tiles[index ^ hop]
+        done.append(lax.ppermute(sent, axis, [(i, i ^ hop) for i in range(size)]))
+    tiles = jnp.stack(done)[index ^ jnp.arange(size)]
+    return joined_along(tiles, concat_dim)
 
 
 def with_halo(cells, sides, width):
@@ -140,7 +163,7 @@
     returning = jnp.einsum("sxbdy,acy->sabxdc", partial_value, grid_y, precision=PRECISE)
     returning = returning.reshape(2, blocks, 1, width_x * cells_z * cells_y)
     table_back = table_x.reshape(blocks, width_x, cells_x)
-    received = lax.all_to_all(returning, ("gy", "gz"), split_axis=1, concat_axis=2, tiled=True)
+    received = exchange_in_pairs(returning, ("gy", "gz"), 1, 2)
     count = received.shape[0]
     pieces = received.reshape(count, blocks, width_x, cells_z, cells_y)
     summed_field = jnp.einsum("sqxdc,qxk->scdk", pieces, table_back, precision=PRECISE)

time: 558 us -> 587 us (1.052)
  waiting for transfers between devices: 116 us -> 71.3 us
  local copies, waits for them, and re-layouts: 77.4 us -> 116 us
  starting transfers between devices: 33.4 us -> 68.1 us
    ppermute x0 -> x15, starting transfers between devices: none -> 54.4 us  [exchange_in_pairs(): done.append(lax.ppermute(sent, axis, [(i, i ^ hop) for i in range(size)]))]
    all_to_all x1 -> x0, waiting for transfers between devices: 41.7 us -> none  [body(): lax.all_to_all(returning, ('gy', 'gz'), split_axis=1, concat_axis=2, tile...]
    all_to_all x1, waiting for transfers between devices: 71 us -> 35.1 us  [body(): lax.all_to_all(outgoing, ('gy', 'gz'), split_axis=1, concat_axis=2, tiled...]
    ppermute x0 -> x15, waiting for transfers between devices: none -> 33.4 us  [exchange_in_pairs(): done.append(lax.ppermute(sent, axis, [(i, i ^ hop) for i in range(size)]))]
    another operation x0 -> x4, local copies, waits for them, and re-layouts: none -> 29.1 us
    all_to_all x1 -> x0, starting transfers between devices: 19.7 us -> none  [body(): lax.all_to_all(returning, ('gy', 'gz'), split_axis=1, concat_axis=2, tile...]
    reshape x3 -> x0, local copies, waits for them, and re-layouts: 18.3 us -> none  [the longest x2 11.7 us: body(): returning = returning.reshape(2, blocks, 1, width_x * cells_z * cells_y)]
    unnamed x17 -> x47, local copies, waits for them, and re-layouts: 27.2 us -> 41.3 us
  transfers between devices with their start and end apart: 6 -> 20, of which waited for: 4 -> 8; matrix products, arithmetic and copies ran while one was open for 7% -> 9% of each run, Pallas kernels for 0% -> 0%
where the time goes in v1:
time: 587 us; the launch traced here: 579 us
  matrix products  219 us (37%)
  local copies, waits for them, and re-layouts  116 us (20%)
  waiting for transfers between devices  71.3 us (12%)
  starting transfers between devices  68.1 us (12%)
  other arithmetic  50.3 us (9%)
  blocking collectives  46.4 us (8%)
  between operations  7.31 us (1%)
    dot_general x1, matrix products, body(): jnp.einsum('isyzx,jsyzx->ij', stacked, stacked, precision=PRECISE)  76.1 us
    ppermute x15, starting transfers between devices, exchange_in_pairs(): done.append(lax.ppermute(sent, axis, [(i, i ^ hop) for i in range(size)]))  54.4 us
    dot_general x1, matrix products, body(): jnp.einsum('i,isyzx->syzx', mixing[1:], past_indirect + MIX_STEP * past_r...  46.6 us
    psum x1, blocking collectives, body(): gram_matrix = lax.psum(gram_matrix, ('gy', 'gz'))  46.4 us
    unnamed x47, local copies, waits for them, and re-layouts  41.3 us
    all_to_all x1, waiting for transfers between devices, body(): lax.all_to_all(outgoing, ('gy', 'gz'), split_axis=1, concat_axis=2, tiled...  35.1 us
    ppermute x15, waiting for transfers between devices, exchange_in_pairs(): done.append(lax.ppermute(sent, axis, [(i, i ^ hop) for i in range(size)]))  33.4 us
    dot_general x1, matrix products, body(): jnp.einsum('sqxdc,qxk->scdk', pieces, table_back, precision=PRECISE)  26.6 us
  transfers between devices with their start and end apart: 20, of which 8 were waited for; matrix products, arithmetic and copies ran while one was open for 9% of the time, Pallas kernels for 0%

profile of v1, /device:TPU:0, one launch (start us, length us, event | category | flops | bytes accessed | tf_op | source)
XLA Modules:
  0.0 578.9 jit_solution(2546400152684250464)
XLA Ops:
  13.1 18.8 %fusion.6 = f32[2,128,8,512]{3,1,2,0:T(8,128)S(1)} fusion(f32[8,1152]{1,0:T(8,128)S(1)} %fusion.224, f32[2,128,1152]{2,1,0:T(8,128)S(1)} %broadcast_multiply_fusion, f32[1152]{0:T(1024)S(1)} %sub.111, f32[512]{0:T(512)S(1)} %iota_convert_fusion), kind=kOutput, calls=%fused_computation.9 | convolution fusion | flops 14503182336 | bytes 5417472 | tf_op jit(solution)/shard_map/sra,xa->srx/dot_general | solution.py:106
  32.0 14.3 %fusion.56 = f32[2,16,32,8,128]{4,2,3,0,1:T(8,128)S(1)} fusion(f32[2,128,8,512]{3,1,2,0:T(8,128)S(1)} %fusion.6, f32[2,128,8,512]{3,2,1,0:T(8,128)S(1)} %copy-done.2, s32[16,32]{1,0:T(8,128)S(1)} %multiply_add_fusion.3), kind=kOutput, calls=%fused_computation.69 | convolution fusion | flops 6451888128 | bytes 12584960 | tf_op jit(solution)/shard_map/scdx,xqk->sqkdc/dot_general | solution.py:144
  58.0 6.8 %all-to-all-start = ((f32[2,16,1,32768]{3,0,2,1:T(2,128)}), f32[2,16,1,32768]{3,0,2,1:T(2,128)}, u32[]{:S(2)}, u32[]{:S(2)}) async-start(f32[2,16,1,32768]{3,0,2,1:T(2,128)} %reshape.488), calls=%async_computation | async-start | bytes 8388608 | tf_op jit(solution)/shard_map/all_to_all | solution.py:148
  70.6 18.3 %copy.84 = f32[4,2,128,8,512]{2,0,3,4,1:T(4,128)} copy(f32[4,2,128,8,512]{4,3,2,1,0:T(8,128)} %param.10) | data formatting | bytes 33554432 | tf_op args[2]
  89.7 17.5 %multiply_add_fusion = f32[4,2,128,8,512]{4,3,2,1,0:T(8,128)} fusion(f32[4,2,128,8,512]{4,3,2,1,0:T(8,128)} %param.9, f32[4,2,128,8,512]{4,3,2,1,0:T(8,128)} %param.10), kind=kLoop, calls=%fused_computation.7 | loop fusion | flops 8388608 | bytes 50331648 | tf_op jit(solution)/shard_map/add | solution.py:180
  107.2 35.1 %all-to-all-done = f32[2,16,1,32768]{3,0,2,1:T(2,128)} async-done(((f32[2,16,1,32768]{3,0,2,1:T(2,128)}), f32[2,16,1,32768]{3,0,2,1:T(2,128)}, u32[]{:S(2)}, u32[]{:S(2)}) %all-to-all-start) | async-done | bytes 4194336 | tf_op jit(solution)/shard_map/all_to_all | solution.py:148
  142.3 6.8 %reshape.489 = f32[2,4,4,32,8,128]{5,4,3,0,2,1:T(8,128)} reshape(f32[2,16,1,32768]{3,0,2,1:T(2,128)} %all-to-all-done) | data formatting | bytes 8388608 | tf_op jit(solution)/shard_map/reshape | solution.py:150
  149.1 13.7 %fusion.21 = f32[2,4,32,8,512,1]{4,3,5,1,2,0:T(8,128)S(1)} fusion(f32[2,4,4,32,8,128]{5,4,3,0,2,1:T(8,128)} %reshape.489, s32[4,128]{1,0:T(4,128)S(1)} %multiply_add_fusion.5), kind=kOutput, calls=%fused_computation.27 | convolution fusion | flops 6446645248 | bytes 8390656 | tf_op jit(solution)/shard_map/sabxdc,acy->sbxdy/dot_general | solution.py:151
  167.4 12.9 %fusion.101 = f32[1,32,32,512]{3,2,1,0:T(8,128)S(1)} fusion(f32[2,32,32,512]{3,2,1,0:T(8,128)S(1)} %fusion.59, f32[]{:T(128)} %bitcast.42, f32[]{:T(128)} %bitcast.41, f32[]{:T(128)} %bitcast.40, f32[]{:T(128)} %bitcast.39, f32[]{:T(128)} %bitcast.14, f32[]{:T(128)} %bitcast.12, f32[]{:T(128)} %bitcast.10, f32[]{:T(128)} %bitcast.8, f32[512]{0:T(512)S(1)} %fusion.246, ...), kind=kLoop, calls=%fused_computation.108 | loop fusion | flops 50331648 | bytes 6297648 | tf_op jit(solution)/shard_map/stack | solution.py:82
  180.2 10.6 %fusion.90 = f32[1,32,32,512]{3,2,1,0:T(8,128)S(1)} fusion(f32[2,32,32,512]{3,2,1,0:T(8,128)S(1)} %fusion.59, f32[]{:T(128)} %bitcast.14, f32[]{:T(128)} %bitcast.13, f32[]{:T(128)} %bitcast.12, f32[]{:T(128)} %bitcast.11, f32[]{:T(128)} %bitcast.10, f32[]{:T(128)} %bitcast.9, f32[]{:T(128)} %bitcast.8, f32[512]{0:T(512)S(1)} %fusion.246, ...), kind=kLoop, calls=%fused_computation.97 | loop fusion | flops 31457280 | bytes 6297648 | tf_op jit(solution)/shard_map/stack | solution.py:82
  195.0 13.3 %fusion.63 = f32[2,4,4,32,8,128]{5,3,4,2,0,1:T(8,128)S(1)} fusion(f32[2,32,4,8,512]{4,3,1,0,2:T(8,128)S(1)} %fusion.62, s32[4,128]{1,0:T(4,128)S(1)} %multiply_add_fusion.5), kind=kOutput, calls=%fused_computation.72 | convolution fusion | flops 6446645248 | bytes 8390656 | tf_op jit(solution)/shard_map/sxbdy,acy->sabxdc/dot_general | solution.py:163
  219.1 16.8 %constant_dynamic-slice_fusion = (f32[2,1,1,1,32768]{4,1,0,3,2:T(1,128)S(1)}, f32[2,1,1,1,32768]{4,1,0,3,2:T(1,128)S(1)}, f32[2,1,1,1,32768]{4,1,0,3,2:T(1,128)S...) fusion(f32[2,16,1,1,32768]{4,1,0,3,2:T(8,128)} %reshape_reshape, ...), kind=kLoop, calls=%fused_computation.309 | loop fusion | bytes 8388672 | tf_op jit(solution)/shard_map/dynamic-slice.15
  238.2 6.3 %collective-permute-start.5 = (f32[2,1,1,32768]{3,0,2,1:T(2,128)S(1)}, f32[2,1,1,32768]{3,0,2,1:T(2,128)S(1)}, u32[]{:S(2)}, u32[]{:S(2)}) collective-permute-start(f32[2,1,1,32768]{3,0,2,1:T(2,128)S(1)} %bitcast.251), channel_id=1, source_target_pairs={{0,2},{1,3},{2,0},{3,1},{4,6},{5,7},{6,4},{7,5},{8,10},{9,11},{10,... | collective-permute-start | bytes 786440 | tf_op jit(solution)/shard_map/ppermute | solution.py:32
  245.0 11.3 %collective-permute-start.7 = (f32[2,1,1,32768]{3,0,2,1:T(2,128)S(1)}, f32[2,1,1,32768]{3,0,2,1:T(2,128)S(1)}, u32[]{:S(2)}, u32[]{:S(2)}) collective-permute-start(f32[2,1,1,32768]{3,0,2,1:T(2,128)S(1)} %bitcast.249), channel_id=1, source_target_pairs={{0,4},{1,5},{2,6},{3,7},{4,0},{5,1},{6,2},{7,3},{8,12},{9,13},{10,... | collective-permute-start | bytes 786440 | tf_op jit(solution)/shard_map/ppermute | solution.py:32
  273.8 13.5 %collective-permute-done.9 = f32[2,1,1,32768]{3,0,2,1:T(2,128)S(1)} collective-permute-done((f32[2,1,1,32768]{3,0,2,1:T(2,128)S(1)}, f32[2,1,1,32768]{3,0,2,1:T(2,128)S(1)}, u32[]{:S(2)}, u32[]{:S(2)}) %collective-permute-start.9) | collective-permute-done | bytes 262176 | tf_op jit(solution)/shard_map/ppermute | solution.py:32
  297.7 20.9 %collective-permute-start.17 = (f32[2,1,1,32768]{3,0,2,1:T(2,128)S(1)}, f32[2,1,1,32768]{3,0,2,1:T(2,128)S(1)}, u32[]{:S(2)}, u32[]{:S(2)}) collective-permute-start(f32[2,1,1,32768]{3,0,2,1:T(2,128)S(1)} %bitcast.239), channel_id=1, source_target_pairs={{0,14},{1,15},{2,12},{3,13},{4,10},{5,11},{6,8},{7,9},{8,6},{9,7},... | collective-permute-start | bytes 786440 | tf_op jit(solution)/shard_map/ppermute | solution.py:32
  319.3 7.6 %collective-permute-done.13 = f32[2,1,1,32768]{3,0,2,1:T(2,128)S(1)} collective-permute-done((f32[2,1,1,32768]{3,0,2,1:T(2,128)S(1)}, f32[2,1,1,32768]{3,0,2,1:T(2,128)S(1)}, u32[]{:S(2)}, u32[]{:S(2)}) %collective-permute-start.13) | collective-permute-done | bytes 262176 | tf_op jit(solution)/shard_map/ppermute | solution.py:32
  338.5 8.6 %gather_fusion = f32[16,2,32768]{2,1,0:T(2,128)} fusion(f32[16,2,32768]{2,1,0:T(2,128)} %bitcast.63, s32[1024]{0:T(1024)S(1)} %pad_clamp_fusion), kind=kCustom, calls=%fused_computation | custom fusion | bytes 8388672 | tf_op jit(solution)/shard_map/gather | solution.py:33
  347.1 6.6 %reshape.490 = f32[2,16,32,8,128]{4,3,2,0,1:T(8,128)} reshape(f32[2,1,16,1,32768]{4,0,2,3,1:T(2,128)} %bitcast.237) | data formatting | bytes 8388608 | tf_op jit(solution)/shard_map/reshape;reshape | solution.py:168
  353.7 26.6 %fusion.14 = f32[2,128,8,512]{3,1,2,0:T(8,128)S(1)} fusion(f32[2,128,8,512]{3,2,1,0:T(8,128)} %param.8, f32[2,128,8,512]{3,1,2,0:T(8,128)} %copy-done.6, f32[2,16,32,8,128]{4,3,2,0,1:T(8,128)} %reshape.490, s32[16,32]{1,0:T(8,128)S(1)} %multiply_add_fusion.3), kind=kOutput, calls=%fused_computation.19 | convolution fusion | flops 6453985280 | bytes 16779264 | tf_op jit(solution)/shard_map/sqxdc,qxk->scdk/dot_general | solution.py:169
  384.8 11.0 %copy.83 = f32[1,2,128,8,512]{2,0,3,4,1:T(1,128)} copy(f32[1,2,128,8,512]{4,2,3,1,0:T(8,128)} %bitcast.236) | data formatting | bytes 8388608 | tf_op jit(solution)/shard_map/broadcast_in_dim | solution.py:171
  395.8 76.1 %fusion.132 = f32[5,5]{0,1:T(8,128)S(1)} fusion(f32[4,2,128,8,512]{2,0,3,4,1:T(4,128)} %copy.84, f32[1,2,128,8,512]{2,0,3,4,1:T(1,128)} %copy.83), kind=kOutput, calls=%fused_computation.159 | convolution fusion | flops 319815680 | bytes 20971620 | tf_op jit(solution)/shard_map/isyzx,jsyzx->ij/dot_general | solution.py:172
  471.9 46.4 %psum.7 = f32[5,5]{0,1:T(8,128)S(1)} all-reduce(f32[5,5]{0,1:T(8,128)S(1)} %fusion.132), channel_id=1, replica_groups=mesh['groups'=2,'gy'=4,'gz'=4] {'gy','gz'}, use_global_device_ids=true, to_apply=%region_0.2 | all-reduce | flops 25 | bytes 200 | tf_op jit(solution)/shard_map/psum | solution.py:173
  522.2 46.6 %fusion.4 = f32[1,2,128,8,512]{4,0,3,2,1:T(1,128)S(1)} fusion(f32[4,2,128,8,512]{4,3,2,1,0:T(8,128)} %multiply_add_fusion, f32[5]{0:T(128)S(1)} %broadcast_divide_fusion), kind=kOutput, calls=%fused_computation.5 | convolution fusion | flops 50331648 | bytes 20971540 | tf_op jit(solution)/shard_map/i,isyzx->syzx/dot_general | solution.py:179
  (125 shorter events, 105.3 us)
Async XLA Ops:
  2.7 6.7 %collective-permute-start = (f32[5,1,1,128]{3,2,1,0:T(1,128)S(1)}, f32[5,1,1,128]{3,2,1,0:T(1,128)S(1)}, u32[]{:S(2)}, u32[]{:S(2)}) collective-permute-start(f32[5,1,1,128]{3,2,1,0:T(1,128)S(1)} %pad_maximum_fusion.5), channel_id=1, source_target_pairs={{0,4},{4,8},{8,12},{12,0},{1,5},{5,9},{9,13},{13,1},{2,6},{6,10},{... | collective-permute-start | bytes 7688 | tf_op jit(solution)/shard_map/ppermute | solution.py:44
  5.7 3.6 collective-permute-start.1
  9.3 3.1 collective-permute-start.2
  9.4 3.1 collective-permute-start.3
  13.1 18.8 %copy-start.2 = (f32[2,128,8,512]{3,2,1,0:T(8,128)S(1)}, f32[2,128,8,512]{3,2,1,0:T(8,128)}, u32[]{:S(2)}) copy-start(f32[2,128,8,512]{3,2,1,0:T(8,128)} %param.8) | copy-start | bytes 12582916
  58.0 84.3 %all-to-all-start = ((f32[2,16,1,32768]{3,0,2,1:T(2,128)}), f32[2,16,1,32768]{3,0,2,1:T(2,128)}, u32[]{:S(2)}, u32[]{:S(2)}) async-start(f32[2,16,1,32768]{3,0,2,1:T(2,128)} %reshape.488), calls=%async_computation | async-start | bytes 8388608 | tf_op jit(solution)/shard_map/all_to_all | solution.py:148
  70.5 18.4 %copy-start.4 = (f32[3,4]{1,0:T(4,128)S(1)}, f32[3,4]{1,0:T(4,128)}, u32[]{:S(2)}) copy-start(f32[3,4]{1,0:T(4,128)} %param.13) | copy-start | bytes 148
  236.1 22.6 %collective-permute-start.4 = (f32[2,1,1,32768]{3,0,2,1:T(2,128)S(1)}, f32[2,1,1,32768]{3,0,2,1:T(2,128)S(1)}, u32[]{:S(2)}, u32[]{:S(2)}) collective-permute-start(f32[2,1,1,32768]{3,0,2,1:T(2,128)S(1)} %bitcast.252), channel_id=1, source_target_pairs={{0,1},{1,0},{2,3},{3,2},{4,5},{5,4},{6,7},{7,6},{8,9},{9,8},{10,11... | collective-permute-start | bytes 786440 | tf_op jit(solution)/shard_map/ppermute | solution.py:32
  238.2 24.1 %collective-permute-start.5 = (f32[2,1,1,32768]{3,0,2,1:T(2,128)S(1)}, f32[2,1,1,32768]{3,0,2,1:T(2,128)S(1)}, u32[]{:S(2)}, u32[]{:S(2)}) collective-permute-start(f32[2,1,1,32768]{3,0,2,1:T(2,128)S(1)} %bitcast.251), channel_id=1, source_target_pairs={{0,2},{1,3},{2,0},{3,1},{4,6},{5,7},{6,4},{7,5},{8,10},{9,11},{10,... | collective-permute-start | bytes 786440 | tf_op jit(solution)/shard_map/ppermute | solution.py:32
  244.7 18.4 %collective-permute-start.6 = (f32[2,1,1,32768]{3,0,2,1:T(2,128)S(1)}, f32[2,1,1,32768]{3,0,2,1:T(2,128)S(1)}, u32[]{:S(2)}, u32[]{:S(2)}) collective-permute-start(f32[2,1,1,32768]{3,0,2,1:T(2,128)S(1)} %bitcast.250), channel_id=1, source_target_pairs={{0,3},{1,2},{2,1},{3,0},{4,7},{5,6},{6,5},{7,4},{8,11},{9,10},{10,... | collective-permute-start | bytes 786440 | tf_op jit(solution)/shard_map/ppermute | solution.py:32
  245.0 24.8 %collective-permute-start.7 = (f32[2,1,1,32768]{3,0,2,1:T(2,128)S(1)}, f32[2,1,1,32768]{3,0,2,1:T(2,128)S(1)}, u32[]{:S(2)}, u32[]{:S(2)}) collective-permute-start(f32[2,1,1,32768]{3,0,2,1:T(2,128)S(1)} %bitcast.249), channel_id=1, source_target_pairs={{0,4},{1,5},{2,6},{3,7},{4,0},{5,1},{6,2},{7,3},{8,12},{9,13},{10,... | collective-permute-start | bytes 786440 | tf_op jit(solution)/shard_map/ppermute | solution.py:32
  256.5 14.3 %collective-permute-start.8 = (f32[2,1,1,32768]{3,0,2,1:T(2,128)S(1)}, f32[2,1,1,32768]{3,0,2,1:T(2,128)S(1)}, u32[]{:S(2)}, u32[]{:S(2)}) collective-permute-start(f32[2,1,1,32768]{3,0,2,1:T(2,128)S(1)} %bitcast.248), channel_id=1, source_target_pairs={{0,5},{1,4},{2,7},{3,6},{4,1},{5,0},{6,3},{7,2},{8,13},{9,12},{10,... | collective-permute-start | bytes 786440 | tf_op jit(solution)/shard_map/ppermute | solution.py:32
  258.7 28.7 %collective-permute-start.9 = (f32[2,1,1,32768]{3,0,2,1:T(2,128)S(1)}, f32[2,1,1,32768]{3,0,2,1:T(2,128)S(1)}, u32[]{:S(2)}, u32[]{:S(2)}) collective-permute-start(f32[2,1,1,32768]{3,0,2,1:T(2,128)S(1)} %bitcast.247), channel_id=1, source_target_pairs={{0,6},{1,7},{2,4},{3,5},{4,2},{5,3},{6,0},{7,1},{8,14},{9,15},{10,... | collective-permute-start | bytes 786440 | tf_op jit(solution)/shard_map/ppermute | solution.py:32
  262.4 30.6 %collective-permute-start.10 = (f32[2,1,1,32768]{3,0,2,1:T(2,128)S(1)}, f32[2,1,1,32768]{3,0,2,1:T(2,128)S(1)}, u32[]{:S(2)}, u32[]{:S(2)}) collective-permute-start(f32[2,1,1,32768]{3,0,2,1:T(2,128)S(1)} %bitcast.246), channel_id=1, source_target_pairs={{0,7},{1,6},{2,5},{3,4},{4,3},{5,2},{6,1},{7,0},{8,15},{9,14},{10,... | collective-permute-start | bytes 786440 | tf_op jit(solution)/shard_map/ppermute | solution.py:32
  263.1 32.3 %collective-permute-start.11 = (f32[2,1,1,32768]{3,0,2,1:T(2,128)S(1)}, f32[2,1,1,32768]{3,0,2,1:T(2,128)S(1)}, u32[]{:S(2)}, u32[]{:S(2)}) collective-permute-start(f32[2,1,1,32768]{3,0,2,1:T(2,128)S(1)} %bitcast.245), channel_id=1, source_target_pairs={{0,8},{1,9},{2,10},{3,11},{4,12},{5,13},{6,14},{7,15},{8,0},{9,1},... | collective-permute-start | bytes 786440 | tf_op jit(solution)/shard_map/ppermute | solution.py:32
  269.8 27.9 %collective-permute-start.12 = (f32[2,1,1,32768]{3,0,2,1:T(2,128)S(1)}, f32[2,1,1,32768]{3,0,2,1:T(2,128)S(1)}, u32[]{:S(2)}, u32[]{:S(2)}) collective-permute-start(f32[2,1,1,32768]{3,0,2,1:T(2,128)S(1)} %bitcast.244), channel_id=1, source_target_pairs={{0,9},{1,8},{2,11},{3,10},{4,13},{5,12},{6,15},{7,14},{8,1},{9,0},... | collective-permute-start | bytes 786440 | tf_op jit(solution)/shard_map/ppermute | solution.py:32
  270.7 56.1 %collective-permute-start.13 = (f32[2,1,1,32768]{3,0,2,1:T(2,128)S(1)}, f32[2,1,1,32768]{3,0,2,1:T(2,128)S(1)}, u32[]{:S(2)}, u32[]{:S(2)}) collective-permute-start(f32[2,1,1,32768]{3,0,2,1:T(2,128)S(1)} %bitcast.243), channel_id=1, source_target_pairs={{0,10},{1,11},{2,8},{3,9},{4,14},{5,15},{6,12},{7,13},{8,2},{9,3},... | collective-permute-start | bytes 786440 | tf_op jit(solution)/shard_map/ppermute | solution.py:32
  287.4 44.4 %collective-permute-start.14 = (f32[2,1,1,32768]{3,0,2,1:T(2,128)S(1)}, f32[2,1,1,32768]{3,0,2,1:T(2,128)S(1)}, u32[]{:S(2)}, u32[]{:S(2)}) collective-permute-start(f32[2,1,1,32768]{3,0,2,1:T(2,128)S(1)} %bitcast.242), channel_id=1, source_target_pairs={{0,11},{1,10},{2,9},{3,8},{4,15},{5,14},{6,13},{7,12},{8,3},{9,2},... | collective-permute-start | bytes 786440 | tf_op jit(solution)/shard_map/ppermute | solution.py:32
  293.0 39.5 %collective-permute-start.15 = (f32[2,1,1,32768]{3,0,2,1:T(2,128)S(1)}, f32[2,1,1,32768]{3,0,2,1:T(2,128)S(1)}, u32[]{:S(2)}, u32[]{:S(2)}) collective-permute-start(f32[2,1,1,32768]{3,0,2,1:T(2,128)S(1)} %bitcast.241), channel_id=1, source_target_pairs={{0,12},{1,13},{2,14},{3,15},{4,8},{5,9},{6,10},{7,11},{8,4},{9,5},... | collective-permute-start | bytes 786440 | tf_op jit(solution)/shard_map/ppermute | solution.py:32
  295.4 37.8 %collective-permute-start.16 = (f32[2,1,1,32768]{3,0,2,1:T(2,128)S(1)}, f32[2,1,1,32768]{3,0,2,1:T(2,128)S(1)}, u32[]{:S(2)}, u32[]{:S(2)}) collective-permute-start(f32[2,1,1,32768]{3,0,2,1:T(2,128)S(1)} %bitcast.240), channel_id=1, source_target_pairs={{0,13},{1,12},{2,15},{3,14},{4,9},{5,8},{6,11},{7,10},{8,5},{9,4},... | collective-permute-start | bytes 786440 | tf_op jit(solution)/shard_map/ppermute | solution.py:32
  297.7 36.2 %collective-permute-start.17 = (f32[2,1,1,32768]{3,0,2,1:T(2,128)S(1)}, f32[2,1,1,32768]{3,0,2,1:T(2,128)S(1)}, u32[]{:S(2)}, u32[]{:S(2)}) collective-permute-start(f32[2,1,1,32768]{3,0,2,1:T(2,128)S(1)} %bitcast.239), channel_id=1, source_target_pairs={{0,14},{1,15},{2,12},{3,13},{4,10},{5,11},{6,8},{7,9},{8,6},{9,7},... | collective-permute-start | bytes 786440 | tf_op jit(solution)/shard_map/ppermute | solution.py:32
  326.9 10.9 %collective-permute-start.18 = (f32[2,1,1,32768]{3,0,2,1:T(2,128)S(1)}, f32[2,1,1,32768]{3,0,2,1:T(2,128)S(1)}, u32[]{:S(2)}, u32[]{:S(2)}) collective-permute-start(f32[2,1,1,32768]{3,0,2,1:T(2,128)S(1)} %bitcast.238), channel_id=1, source_target_pairs={{0,15},{1,14},{2,13},{3,12},{4,11},{5,10},{6,9},{7,8},{8,7},{9,6},... | collective-permute-start | bytes 786440 | tf_op jit(solution)/shard_map/ppermute | solution.py:32
  522.2 46.7 %copy-start.1 = (f32[2,128,8,512]{3,1,2,0:T(8,128)S(1)}, f32[2,128,8,512]{3,1,2,0:T(8,128)}, u32[]{:S(2)}) copy-start(f32[2,128,8,512]{3,1,2,0:T(8,128)} %copy-done) | copy-start | bytes 12582916
  522.2 46.7 %copy-start.3 = (f32[2,128,8,512]{3,2,1,0:T(8,128)S(1)}, f32[2,128,8,512]{3,2,1,0:T(8,128)}, u32[]{:S(2)}) copy-start(f32[2,128,8,512]{3,2,1,0:T(8,128)} %param.8) | copy-start | bytes 12582916
  (3 other events, 25.6 us)
